TPU v7x, 128 devices: a whole 4x4x4 slice. The times are simulated.
128 devices in a mesh: arc: 16 (over x, z), vec: 8 (over y, core).
Axes of the slice: x: 4, y: 4, z: 4, core: 2. Of those that a mesh axis runs over, the one named last changes fastest.
Arguments:
- right_side: float32 [640, 128, 128], P(('arc', 'vec')), may hold values from -6 to 6
- prior_diag: float32 [640, 128], P(('arc', 'vec')), may hold values from 0.5 to 4
- inv_factor: bfloat16 [2048, 256, 256], P(('arc', 'vec'))
- coupling_panel: bfloat16 [2048, 256, 1024], P(('arc', 'vec')), may hold values from -0.09375 to 0.09375
- coupling_owner: int32 [2048, 8], replicated, may hold values from 0 to 127, all different within a row; in each aligned block of 16 rows (0 to 15, 16 to 31, ...) at most 2 rows name the same one
- coupling_block: int32 [2048, 8], replicated, may hold values from 0 to 4
Outputs:
- solution_field: float32 [640, 128, 128], P(('arc', 'vec'))
- residual: float32 [640, 128, 128], P(('arc', 'vec'))
Inputs may be any that keep to these rules, and one draw needn't show every extreme that they name: `coupling_owner`: the 8 holders named for one arc are different. Among the 16 arcs of one device (aligned blocks of rows) no holder is named more than 2 times; some holder is named exactly 2 times.
All inputs are finite; a program needn't handle non-finite values.
Results may differ from a plain program's by a relative error of at most 0.006.
The roundings to bfloat16 on the way count: a program that leaves them out, or rounds other values in their place, can miss the bound.
Values may be sent and summed in bfloat16 or wider, within the bound.
A program may use at most 128 MiB of HBM per device.

v0:
```python
import jax
import jax.numpy as jnp
from jax import lax
from jax.sharding import PartitionSpec as P

ITERS = 2


def inner_gram(left, right):
    return jnp.einsum("grc,grd->cd", left, right, precision=lax.Precision.HIGHEST)


def combine_cols(field, weights):
    return jnp.einsum("grc,cd->grd", field, weights, precision=lax.Precision.HIGHEST)


def trade_out(buffer):
    return lax.all_to_all(buffer, ("arc", "vec"), split_axis=0, concat_axis=0, tiled=True)


def trade_back(buffer):
    return lax.all_to_all(buffer, ("arc", "vec"), split_axis=0, concat_axis=0, tiled=True)


def per_device(right_side, prior_diag, inv_factor, coupling_panel, coupling_owner, coupling_block):
    device_count = lax.axis_size(("arc", "vec"))
    my_index = lax.axis_index(("arc", "vec"))
    arcs_here = coupling_panel.shape[0]
    links = coupling_owner.shape[1]
    blocks_here = right_side.shape[0]
    block_rows = right_side.shape[1]
    rhs_count = right_side.shape[2]
    entries = arcs_here * links
    slot_count = (entries + device_count - 1) // device_count + 1
    owner_all = coupling_owner.reshape(device_count, entries)
    block_all = coupling_block.reshape(device_count, entries)
    position = jnp.arange(entries, dtype=jnp.int32)
    earlier = (owner_all[:, :, None] == owner_all[:, None, :]) & (
        position[None, None, :] < position[None, :, None]
    )
    rank_all = jnp.sum(earlier.astype(jnp.int32), axis=2)
    owner_mine = lax.dynamic_index_in_dim(owner_all, my_index, 0, keepdims=False)
    rank_mine = lax.dynamic_index_in_dim(rank_all, my_index, 0, keepdims=False)
    slot_mine = owner_mine * slot_count + rank_mine
    slot_ids = jnp.arange(slot_count, dtype=jnp.int32)
    matches = (owner_all[:, None, :] == my_index) & (
        rank_all[:, None, :] == slot_ids[None, :, None]
    )
    filled = jnp.any(matches, axis=2).reshape(-1)
    source_block = jnp.sum(jnp.where(matches, block_all[:, None, :], 0), axis=2).reshape(-1)
    block_ids = jnp.arange(blocks_here, dtype=jnp.int32)
    selector = ((source_block[:, None] == block_ids[None, :]) & filled[:, None]).astype(
        jnp.bfloat16
    )
    solution_field = jnp.zeros_like(right_side)
    residual = right_side
    direction = right_side
    res_gram = lax.psum(inner_gram(residual, residual), ("arc", "vec"))
    for sweep_index in range(ITERS):
        local_rounded = direction.astype(jnp.bfloat16)
        outgoing = jnp.where(
            filled[:, None, None], local_rounded[source_block], jnp.zeros((), jnp.bfloat16)
        )
        arrived = trade_out(outgoing)
        fetched = arrived[slot_mine].reshape(arcs_here, links * block_rows, rhs_count)
        coupled = jnp.einsum(
            "apk,akc->apc", coupling_panel, fetched, preferred_element_type=jnp.float32
        ).astype(jnp.bfloat16)
        whitened = jnp.einsum(
            "apq,aqc->apc", inv_factor, coupled, preferred_element_type=jnp.float32
        ).astype(jnp.bfloat16)
        smoothed = jnp.einsum(
            "aqp,aqc->apc", inv_factor, whitened, preferred_element_type=jnp.float32
        ).astype(jnp.bfloat16)
        projected = jnp.einsum(
            "apk,apc->akc", coupling_panel, smoothed, preferred_element_type=jnp.float32
        ).astype(jnp.bfloat16)
        projected = projected.reshape(entries, block_rows, rhs_count)
        returning = (
            jnp.zeros((device_count * slot_count, block_rows, rhs_count), jnp.bfloat16)
            .at[slot_mine]
            .set(projected)
        )
        came_back = trade_back(returning)
        summed = jnp.einsum("sb,src->brc", selector, came_back, preferred_element_type=jnp.float32)
        image_vec = prior_diag[:, :, None] * direction + summed
        curv_gram = lax.psum(inner_gram(direction, image_vec), ("arc", "vec"))
        factor_low = jnp.linalg.cholesky(curv_gram)
        step_mat = jax.scipy.linalg.cho_solve((factor_low, True), res_gram)
        solution_field = solution_field + combine_cols(direction, step_mat)
        residual = residual - combine_cols(image_vec, step_mat)
        if sweep_index + 1 < ITERS:
            new_gram = lax.psum(inner_gram(residual, residual), ("arc", "vec"))
            beta_mat = jax.scipy.linalg.cho_solve((jnp.linalg.cholesky(res_gram), True), new_gram)
            direction = residual + combine_cols(direction, beta_mat)
            res_gram = new_gram
    return (solution_field, residual)


def solution(mesh):
    in_specs = (
        P(("arc", "vec"), None, None),
        P(("arc", "vec"), None),
        P(("arc", "vec"), None, None),
        P(("arc", "vec"), None, None),
        P(),
        P(),
    )
    out_specs = (P(("arc", "vec"), None, None), P(("arc", "vec"), None, None))
    return jax.shard_map(
        per_device, mesh=mesh, in_specs=in_specs, out_specs=out_specs, check_vma=False
    )
```

profile of v0, /device:TPU:1, one launch (start us, length us, event | category | flops | bytes accessed | tf_op | source)
XLA Modules:
  0.0 1105.9 jit_solution(6747091864298645977)
XLA Ops:
  7.2 1.3 copy.134
  9.1 5.1 convert_reduce_fusion
  14.6 1.2 copy.135
  16.7 1.0 convert_element_type.47
  17.7 8.3 gather_fusion
  26.0 7.2 broadcast_select_fusion.1
  33.3 12.3 %all-to-all-start = ((bf16[256,128,128]{2,1,0:T(8,128)(2,1)}), bf16[256,128,128]{2,1,0:T(8,128)(2,1)}, u32[]{:S(2)}, u32[]{:S(2)}) async-start(bf16[256,128,128]{2,1,0:T(8,128)(2,1)} %broadcast_select_fusion.1), calls=%async_computation | async-start | bytes 16777216 | tf_op jit(solution)/shard_map/all_to_all | solution.py:18
  45.7 106.4 %all-to-all-done = bf16[256,128,128]{2,1,0:T(8,128)(2,1)} async-done(((bf16[256,128,128]{2,1,0:T(8,128)(2,1)}), bf16[256,128,128]{2,1,0:T(8,128)(2,1)}, u32[]{:S(2)}, u32[]{:S(2)}) %all-to-all-start) | async-done | bytes 8388640 | tf_op jit(solution)/shard_map/all_to_all | solution.py:18
  152.0 6.4 gather_fusion.1
  158.5 8.2 convolution_convert_fusion.4
  166.7 6.9 convert_bitcast_fusion.1
  173.6 6.4 copy.140
  180.0 5.3 broadcast.116.clone
  185.3 19.4 %scatter_fusion = bf16[256,128,128]{2,1,0:T(8,128)(2,1)} fusion(bf16[256,128,128]{2,1,0:T(8,128)(2,1)} %broadcast.116.clone, s32[128]{0:T(128)S(1)} %fusion.34, bf16[128,128,128]{2,1,0:T(8,128)(2,1)} %bitcast.106), kind=kCustom, calls=%fused_computation.4 | custom fusion | bytes 12583424 | tf_op jit(solution)/shard_map/scatter | solution.py:82
  204.7 6.8 all-to-all-start.1
  211.8 1.3 convolution_bitcast_fusion.7
  213.2 104.7 %all-to-all-done.1 = bf16[256,128,128]{2,1,0:T(8,128)(2,1)} async-done(((bf16[256,128,128]{2,1,0:T(8,128)(2,1)}), bf16[256,128,128]{2,1,0:T(8,128)(2,1)}, u32[]{:S(2)}, u32[]{:S(2)}) %all-to-all-start.1) | async-done | bytes 8388640 | tf_op jit(solution)/shard_map/all_to_all | solution.py:22
  317.9 7.8 fusion.2
  325.7 1.4 convolution_bitcast_fusion.8
  327.5 139.7 %all-reduce.9.cloned.1.call-done = (f32[128,128]{0,1:T(8,128)}, f32[128,128]{0,1:T(8,128)}) async-done(((f32[128,128]{0,1:T(8,128)}, f32[128,128]{0,1:T(8,128)}), (f32[128,128]{0,1:T(8,128)}, f32[128,128]{0,1:T(8,128)})) %all-reduce.9.cloned.1.call-update) | async-done | bytes 131088 | tf_op jit(solution)/shard_map/psum | solution.py:58
  470.0 11.7 %cholesky.70 = f32[128,128]{1,0:T(8,128)S(1)} custom-call(f32[128,128]{1,0:T(8,128)S(1)} %get-tuple-element.18), custom_call_target="Cholesky" | custom-call | tf_op jit(solution)/shard_map/jit(cholesky)/cholesky | solution.py:94
  482.4 11.7 %cholesky.59 = f32[128,128]{1,0:T(8,128)S(1)} custom-call(f32[128,128]{1,0:T(8,128)S(1)} %get-tuple-element.19), custom_call_target="Cholesky" | custom-call | tf_op jit(solution)/shard_map/jit(cholesky)/cholesky | solution.py:88
  495.5 9.8 custom-call.9
  505.3 1.1 fusion.23
  507.1 1.3 convolution_bitcast_fusion.5
  508.4 10.2 all-reduce.7.cloned.1.call-start
  518.7 1.5 fusion.12
  520.1 9.8 custom-call.10
  530.0 114.2 %all-reduce.5.cloned.1.call-done = f32[128,128]{1,0:T(8,128)} async-done(((f32[128,128]{1,0:T(8,128)}), f32[128,128]{1,0:T(8,128)}) %all-reduce.5.cloned.1.call-update) | async-done | bytes 65552 | tf_op jit(solution)/shard_map/psum | solution.py:93
  644.2 1.1 fusion.19
  646.0 8.3 gather_fusion.2
  654.4 7.2 broadcast_select_fusion
  661.6 103.7 %all_to_all.20 = bf16[256,128,128]{2,1,0:T(8,128)(2,1)} all-to-all(bf16[256,128,128]{2,1,0:T(8,128)(2,1)} %broadcast_select_fusion), channel_id=1, replica_groups=mesh['arc'=16,'vec'=8] {'arc','vec'}, dimensions={0} | all-to-all | bytes 16777216 | tf_op jit(solution)/shard_map/all_to_all | solution.py:18
  765.3 6.4 gather_fusion.3
  771.8 9.2 convolution_convert_fusion.1
  781.0 7.2 convert_bitcast_fusion
  788.2 6.4 copy.153
  794.6 5.3 broadcast.116
  799.9 19.4 %scatter_fusion.1 = bf16[256,128,128]{2,1,0:T(8,128)(2,1)} fusion(bf16[256,128,128]{2,1,0:T(8,128)(2,1)} %broadcast.116, s32[128]{0:T(128)S(1)} %fusion.34, bf16[128,128,128]{2,1,0:T(8,128)(2,1)} %bitcast.105), kind=kCustom, calls=%fused_computation.5 | custom fusion | bytes 12583424 | tf_op jit(solution)/shard_map/scatter | solution.py:82
  819.3 106.0 %all_to_all.21 = bf16[256,128,128]{2,1,0:T(8,128)(2,1)S(1)} all-to-all(bf16[256,128,128]{2,1,0:T(8,128)(2,1)} %scatter_fusion.1), channel_id=1, replica_groups=mesh['arc'=16,'vec'=8] {'arc','vec'}, dimensions={0} | all-to-all | bytes 16777216 | tf_op jit(solution)/shard_map/all_to_all | solution.py:22
  925.3 4.5 fusion
  930.5 1.5 convolution_bitcast_fusion.3
  932.0 1.2 convolution_bitcast_fusion.1
  933.2 136.1 %all-reduce.7.cloned.1.call-done = f32[128,128]{0,1:T(8,128)} async-done(((f32[128,128]{0,1:T(8,128)}), f32[128,128]{0,1:T(8,128)}) %all-reduce.7.cloned.1.call-update) | async-done | bytes 65552 | tf_op jit(solution)/shard_map/psum | solution.py:87
  1071.1 11.7 %cholesky.81 = f32[128,128]{1,0:T(8,128)S(1)} custom-call(f32[128,128]{1,0:T(8,128)S(1)} %fusion.17), custom_call_target="Cholesky" | custom-call | tf_op jit(solution)/shard_map/jit(cholesky)/cholesky | solution.py:88
  1084.2 9.8 custom-call.11
  1094.5 2.2 convolution_subtract_fusion
  1096.7 1.5 convolution_add_fusion
  (52 shorter events, 14.1 us)
Async XLA Ops:
  7.2 151.3 %copy-start = (bf16[16,256,256]{2,1,0:T(8,128)(2,1)S(1)}, bf16[16,256,256]{2,1,0:T(8,128)(2,1)}, u32[]{:S(2)}) copy-start(bf16[16,256,256]{2,1,0:T(8,128)(2,1)} %param.11) | copy-start | bytes 6291460
  33.3 118.8 %all-to-all-start = ((bf16[256,128,128]{2,1,0:T(8,128)(2,1)}), bf16[256,128,128]{2,1,0:T(8,128)(2,1)}, u32[]{:S(2)}, u32[]{:S(2)}) async-start(bf16[256,128,128]{2,1,0:T(8,128)(2,1)} %broadcast_select_fusion.1), calls=%async_computation | async-start | bytes 16777216 | tf_op jit(solution)/shard_map/all_to_all | solution.py:18
  204.7 7.2 copy-start.1
  204.7 113.2 %all-to-all-start.1 = ((bf16[256,128,128]{2,1,0:T(8,128)(2,1)}), bf16[256,128,128]{2,1,0:T(8,128)(2,1)}, u32[]{:S(2)}, u32[]{:S(2)}) async-start(bf16[256,128,128]{2,1,0:T(8,128)(2,1)} %scatter_fusion), calls=%async_computation.1 | async-start | bytes 16777216 | tf_op jit(solution)/shard_map/all_to_all | solution.py:22
  211.4 114.3 %copy-start.5 = (f32[5,128]{1,0:T(8,128)S(1)}, f32[5,128]{1,0:T(8,128)}, u32[]{:S(2)}) copy-start(f32[5,128]{1,0:T(8,128)} %param.10) | copy-start | bytes 7684
  211.4 255.8 %all-reduce.9.cloned.1.call-start = ((), (), s32[]{:S(2)}) async-start(), calls=%async_computation.6 | async-start | bytes 262144 | tf_op jit(solution)/shard_map/psum | solution.py:58
  327.2 317.0 %all-reduce.5.cloned.1.call-start = ((), (), s32[]{:S(2)}) async-start(), calls=%async_computation.4 | async-start | bytes 131072 | tf_op jit(solution)/shard_map/psum | solution.py:93
  481.7 13.1 %copy-start.4 = (f32[128,128]{1,0:T(8,128)}, f32[128,128]{1,0:T(8,128)S(1)}, u32[]{:S(2)}) copy-start(f32[128,128]{1,0:T(8,128)S(1)} %cholesky.70) | copy-start | bytes 196612
  508.4 560.9 %all-reduce.7.cloned.1.call-start = ((), (), s32[]{:S(2)}) async-start(), calls=%async_computation.5 | async-start | bytes 131072 | tf_op jit(solution)/shard_map/psum | solution.py:87
  925.3 168.7 %copy-start.3 = (f32[128,128]{1,0:T(8,128)S(1)}, f32[128,128]{1,0:T(8,128)}, u32[]{:S(2)}) copy-start(f32[128,128]{1,0:T(8,128)} %all-reduce.5.cloned.1.call-done) | copy-start | bytes 196612
  929.7 0.8 copy-start.2
Sparse Core Ops, SparseCore 0:
  327.3 139.8 all-reduce.8
  508.6 135.5 all-reduce.4
  932.1 137.1 all-reduce.6
where the time goes:
time: 1110 us
  waiting for transfers between devices  601 us (54%)
  blocking collectives  210 us (19%)
  local copies, waits for them, and re-layouts  100 us (9%)
  other arithmetic  92 us (8%)
  matrix products  58.4 us (5%)
  starting transfers between devices  29.9 us (3%)
  between operations  14.3 us (1%)
    psum x1, waiting for transfers between devices, per_device(): res_gram = lax.psum(inner_gram(residual, residual), ('arc', 'vec'))  140 us
    psum x1, waiting for transfers between devices, per_device(): curv_gram = lax.psum(inner_gram(direction, image_vec), ('arc', 'vec'))  136 us
    psum x1, waiting for transfers between devices, per_device(): new_gram = lax.psum(inner_gram(residual, residual), ('arc', 'vec'))  114 us
    all_to_all x1, waiting for transfers between devices, trade_out(): lax.all_to_all(buffer, ('arc', 'vec'), split_axis=0, concat_axis=0, tiled...  106 us
    all_to_all x1, blocking collectives, trade_back(): lax.all_to_all(buffer, ('arc', 'vec'), split_axis=0, concat_axis=0, tiled...  106 us
    all_to_all x1, waiting for transfers between devices, trade_back(): lax.all_to_all(buffer, ('arc', 'vec'), split_axis=0, concat_axis=0, tiled...  105 us
    all_to_all x1, blocking collectives, trade_out(): lax.all_to_all(buffer, ('arc', 'vec'), split_axis=0, concat_axis=0, tiled...  104 us
    scatter x2, local copies, waits for them, and re-layouts, per_device(): returning = jnp.zeros((device_count * slot_count, block_rows, rhs_count),...  38.7 us
  transfers between devices with their start and end apart: 5, of which 5 were waited for; matrix products, arithmetic and copies ran while one was open for 1% of the time, Pallas kernels for 0%

commit v1 on v0

--- a/solution.py
+++ b/solution.py
@@ -55,7 +55,8 @@
     solution_field = jnp.zeros_like(right_side)
     residual = right_side
     direction = right_side
-    res_gram = lax.psum(inner_gram(residual, residual), ("arc", "vec"))
+    partial = lax.psum(inner_gram(residual, residual), "arc")
+    res_gram = lax.psum(partial, "vec")
     for sweep_index in range(ITERS):
         local_rounded = direction.astype(jnp.bfloat16)
         outgoing = jnp.where(

time: 1110 us -> 1220 us (1.099)
  waiting for transfers between devices: 601 us -> 718 us
    psum x1 -> x2, waiting for transfers between devices: 136 us -> 273 us  [per_device(): curv_gram = lax.psum(inner_gram(direction, image_vec), ('arc', 'vec'))]
    all_to_all x1, waiting for transfers between devices: 105 us -> 0.01 us  [trade_back(): lax.all_to_all(buffer, ('arc', 'vec'), split_axis=0, concat_axis=0, tiled...]
    psum x1 -> x2, waiting for transfers between devices: 140 us -> 216 us  [the longest x1 156 us: per_device(): partial = lax.psum(inner_gram(residual, residual), 'arc')]
  transfers between devices with their start and end apart: 5 -> 7, of which waited for: 5 -> 6; matrix products, arithmetic and copies ran while one was open for 1% -> 2% of each run, Pallas kernels for 0% -> 0%
where the time goes in v1:
time: 1220 us
  waiting for transfers between devices  718 us (59%)
  blocking collectives  211 us (17%)
  local copies, waits for them, and re-layouts  100 us (8%)
  other arithmetic  92.8 us (8%)
  matrix products  57.6 us (5%)
  starting transfers between devices  20.3 us (2%)
  between operations  16.2 us (1%)
    psum x2, waiting for transfers between devices, per_device(): curv_gram = lax.psum(inner_gram(direction, image_vec), ('arc', 'vec'))  273 us
    psum x1, waiting for transfers between devices, per_device(): partial = lax.psum(inner_gram(residual, residual), 'arc')  156 us
    psum x1, waiting for transfers between devices, per_device(): new_gram = lax.psum(inner_gram(residual, residual), ('arc', 'vec'))  123 us
    all_to_all x1, blocking collectives, trade_back(): lax.all_to_all(buffer, ('arc', 'vec'), split_axis=0, concat_axis=0, tiled...  107 us
    all_to_all x1, waiting for transfers between devices, trade_out(): lax.all_to_all(buffer, ('arc', 'vec'), split_axis=0, concat_axis=0, tiled...  106 us
    all_to_all x1, blocking collectives, trade_out(): lax.all_to_all(buffer, ('arc', 'vec'), split_axis=0, concat_axis=0, tiled...  104 us
    psum x1, waiting for transfers between devices, per_device(): res_gram = lax.psum(partial, 'vec')  59.5 us
    scatter x2, local copies, waits for them, and re-layouts, per_device(): returning = jnp.zeros((device_count * slot_count, block_rows, rhs_count),...  38.6 us
  transfers between devices with their start and end apart: 7, of which 6 were waited for; matrix products, arithmetic and copies ran while one was open for 2% of the time, Pallas kernels for 0%

profile of v1, /device:TPU:1, one launch (start us, length us, event | category | flops | bytes accessed | tf_op | source)
XLA Modules:
  0.0 1216.3 jit_solution(4934429302587030647)
XLA Ops:
  8.0 1.3 copy.134
  9.9 5.1 convert_reduce_fusion
  15.4 1.2 copy.135
  17.5 1.0 convert_element_type.47
  18.5 8.3 gather_fusion
  26.9 7.2 broadcast_select_fusion.1
  34.1 12.3 %all-to-all-start = ((bf16[256,128,128]{2,1,0:T(8,128)(2,1)}), bf16[256,128,128]{2,1,0:T(8,128)(2,1)}, u32[]{:S(2)}, u32[]{:S(2)}) async-start(bf16[256,128,128]{2,1,0:T(8,128)(2,1)} %broadcast_select_fusion.1), calls=%async_computation | async-start | bytes 16777216 | tf_op jit(solution)/shard_map/all_to_all | solution.py:18
  46.5 106.4 %all-to-all-done = bf16[256,128,128]{2,1,0:T(8,128)(2,1)} async-done(((bf16[256,128,128]{2,1,0:T(8,128)(2,1)}), bf16[256,128,128]{2,1,0:T(8,128)(2,1)}, u32[]{:S(2)}, u32[]{:S(2)}) %all-to-all-start) | async-done | bytes 8388640 | tf_op jit(solution)/shard_map/all_to_all | solution.py:18
  152.9 6.4 gather_fusion.1
  159.3 8.2 convolution_convert_fusion.4
  167.5 6.9 convert_bitcast_fusion.1
  174.5 6.4 copy.140
  180.9 5.3 broadcast.116.clone
  186.2 19.3 %scatter_fusion = bf16[256,128,128]{2,1,0:T(8,128)(2,1)} fusion(bf16[256,128,128]{2,1,0:T(8,128)(2,1)} %broadcast.116.clone, s32[128]{0:T(128)S(1)} %fusion.34, bf16[128,128,128]{2,1,0:T(8,128)(2,1)} %bitcast.106), kind=kCustom, calls=%fused_computation.4 | custom fusion | bytes 12583424 | tf_op jit(solution)/shard_map/scatter | solution.py:83
  205.5 6.8 all-to-all-start.1
  212.4 1.3 convolution_bitcast_fusion.7
  213.8 156.3 %all-reduce.8.cloned.1.call-done = f32[128,128]{0,1:T(8,128)} async-done(((f32[128,128]{0,1:T(8,128)}), f32[128,128]{0,1:T(8,128)}) %all-reduce.8.cloned.1.call-update) | async-done | bytes 65552 | tf_op jit(solution)/shard_map/psum | solution.py:58
  370.5 59.5 %all-reduce.10.cloned.1.call-done = f32[128,128]{0,1:T(8,128)} async-done(((f32[128,128]{0,1:T(8,128)}), f32[128,128]{0,1:T(8,128)}) %all-reduce.10.cloned.1.call-update) | async-done | bytes 65552 | tf_op jit(solution)/shard_map/psum | solution.py:59
  430.0 1.0 copy.148
  431.9 11.7 cholesky.70
  443.6 7.8 fusion.2
  451.5 1.4 convolution_bitcast_fusion.8
  453.9 137.6 %all-reduce.6.cloned.1.call-done = f32[128,128]{0,1:T(8,128)} async-done(((f32[128,128]{0,1:T(8,128)}), f32[128,128]{0,1:T(8,128)}) %all-reduce.6.cloned.1.call-update) | async-done | bytes 65552 | tf_op jit(solution)/shard_map/psum | solution.py:88
  593.3 11.7 cholesky.59
  606.3 9.8 custom-call.9
  617.1 1.3 convolution_bitcast_fusion.5
  619.0 1.5 fusion.12
  620.5 9.8 custom-call.10
  630.3 122.7 %all-reduce.12.cloned.1.call-done = f32[128,128]{1,0:T(8,128)} async-done(((f32[128,128]{1,0:T(8,128)}), f32[128,128]{1,0:T(8,128)}) %all-reduce.12.cloned.1.call-update) | async-done | bytes 65552 | tf_op jit(solution)/shard_map/psum | solution.py:94
  753.0 1.1 fusion.19
  754.8 8.3 gather_fusion.2
  763.2 7.2 broadcast_select_fusion
  770.4 103.9 %all_to_all.20 = bf16[256,128,128]{2,1,0:T(8,128)(2,1)} all-to-all(bf16[256,128,128]{2,1,0:T(8,128)(2,1)} %broadcast_select_fusion), channel_id=1, replica_groups=mesh['arc'=16,'vec'=8] {'arc','vec'}, dimensions={0} | all-to-all | bytes 16777216 | tf_op jit(solution)/shard_map/all_to_all | solution.py:18
  874.3 6.4 gather_fusion.3
  880.7 9.2 convolution_convert_fusion.1
  890.0 7.2 convert_bitcast_fusion
  897.2 6.4 copy.153
  903.5 5.3 broadcast.116
  908.9 19.4 %scatter_fusion.1 = bf16[256,128,128]{2,1,0:T(8,128)(2,1)} fusion(bf16[256,128,128]{2,1,0:T(8,128)(2,1)} %broadcast.116, s32[128]{0:T(128)S(1)} %fusion.34, bf16[128,128,128]{2,1,0:T(8,128)(2,1)} %bitcast.105), kind=kCustom, calls=%fused_computation.5 | custom fusion | bytes 12583424 | tf_op jit(solution)/shard_map/scatter | solution.py:83
  928.2 106.9 %all_to_all.21 = bf16[256,128,128]{2,1,0:T(8,128)(2,1)S(1)} all-to-all(bf16[256,128,128]{2,1,0:T(8,128)(2,1)} %scatter_fusion.1), channel_id=1, replica_groups=mesh['arc'=16,'vec'=8] {'arc','vec'}, dimensions={0} | all-to-all | bytes 16777216 | tf_op jit(solution)/shard_map/all_to_all | solution.py:22
  1035.1 4.5 fusion
  1040.4 1.5 convolution_bitcast_fusion.3
  1041.8 1.2 convolution_bitcast_fusion.1
  1043.1 135.7 %all-reduce.14.cloned.1.call-done = f32[128,128]{0,1:T(8,128)} async-done(((f32[128,128]{0,1:T(8,128)}), f32[128,128]{0,1:T(8,128)}) %all-reduce.14.cloned.1.call-update) | async-done | bytes 65552 | tf_op jit(solution)/shard_map/psum | solution.py:88
  1180.5 11.7 cholesky.81
  1193.6 9.8 custom-call.11
  1203.9 2.2 convolution_subtract_fusion
  1206.1 1.5 convolution_add_fusion
  (61 shorter events, 14.9 us)
Async XLA Ops:
  8.0 151.3 %copy-start = (bf16[16,256,256]{2,1,0:T(8,128)(2,1)S(1)}, bf16[16,256,256]{2,1,0:T(8,128)(2,1)}, u32[]{:S(2)}) copy-start(bf16[16,256,256]{2,1,0:T(8,128)(2,1)} %param.11) | copy-start | bytes 6291460
  34.1 118.8 %all-to-all-start = ((bf16[256,128,128]{2,1,0:T(8,128)(2,1)}), bf16[256,128,128]{2,1,0:T(8,128)(2,1)}, u32[]{:S(2)}, u32[]{:S(2)}) async-start(bf16[256,128,128]{2,1,0:T(8,128)(2,1)} %broadcast_select_fusion.1), calls=%async_computation | async-start | bytes 16777216 | tf_op jit(solution)/shard_map/all_to_all | solution.py:18
  205.5 6.9 copy-start.1
  205.5 238.1 %all-to-all-start.1 = ((bf16[256,128,128]{2,1,0:T(8,128)(2,1)}), bf16[256,128,128]{2,1,0:T(8,128)(2,1)}, u32[]{:S(2)}, u32[]{:S(2)}) async-start(bf16[256,128,128]{2,1,0:T(8,128)(2,1)} %scatter_fusion), calls=%async_computation.1 | async-start | bytes 16777216 | tf_op jit(solution)/shard_map/all_to_all | solution.py:22
  212.3 239.2 %copy-start.6 = (f32[5,128]{1,0:T(8,128)S(1)}, f32[5,128]{1,0:T(8,128)}, u32[]{:S(2)}) copy-start(f32[5,128]{1,0:T(8,128)} %param.10) | copy-start | bytes 7684
  212.3 157.8 %all-reduce.8.cloned.1.call-start = ((), (), s32[]{:S(2)}) async-start(), calls=%async_computation.5 | async-start | bytes 131072 | tf_op jit(solution)/shard_map/psum | solution.py:58
  213.7 216.3 %all-reduce.10.cloned.1.call-start = ((), (), s32[]{:S(2)}) async-start(), calls=%async_computation.6 | async-start | bytes 131072 | tf_op jit(solution)/shard_map/psum | solution.py:59
  370.1 221.4 %all-reduce.6.cloned.1.call-start = ((), (), s32[]{:S(2)}) async-start(), calls=%async_computation.4 | async-start | bytes 131072 | tf_op jit(solution)/shard_map/psum | solution.py:88
  430.0 186.2 %copy-start.3 = (f32[128,128]{0,1:T(8,128)S(1)}, f32[128,128]{0,1:T(8,128)}, u32[]{:S(2)}) copy-start(f32[128,128]{0,1:T(8,128)} %all-reduce.10.cloned.1.call-done) | copy-start | bytes 196612
  443.6 10.3 copy-start.5
  452.9 300.0 %all-reduce.12.cloned.1.call-start = ((), (), s32[]{:S(2)}) async-start(), calls=%async_computation.7 | async-start | bytes 131072 | tf_op jit(solution)/shard_map/psum | solution.py:94
  618.5 560.2 %all-reduce.14.cloned.1.call-start = ((), (), s32[]{:S(2)}) async-start(), calls=%async_computation.8 | async-start | bytes 131072 | tf_op jit(solution)/shard_map/psum | solution.py:88
  1035.1 168.3 %copy-start.4 = (f32[128,128]{1,0:T(8,128)S(1)}, f32[128,128]{1,0:T(8,128)}, u32[]{:S(2)}) copy-start(f32[128,128]{1,0:T(8,128)} %all-reduce.12.cloned.1.call-done) | copy-start | bytes 196612
  1039.6 0.8 copy-start.2
Sparse Core Ops, SparseCore 0:
  216.9 153.0 all-reduce.7
  372.5 57.4 all-reduce.9
Sparse Core Ops, SparseCore 1:
  453.0 138.4 all-reduce.5
  618.6 134.3 all-reduce.11
  1041.9 136.7 all-reduce.13
